TPU v7x, 256 devices: a whole 4x4x8 slice. The times are simulated.
256 devices in a mesh: row: 8 (over x, core), col: 32 (over y, z).
Axes of the slice: x: 4, y: 4, z: 8, core: 2. Of those that a mesh axis runs over, the one named last changes fastest.
Arguments:
- upper_panel: float32 [2048, 8192], P('row', 'col')
- lower_panel: float32 [2048, 8192], P('row', 'col')
- pole_values: float32 [2, 8192], P(None, 'col'), may hold values from 0 to 4, as said below
- coupling: float32 [2, 8192], P(None, 'col'), may hold values from -6 to 6
- kept_mask: int32 [2, 8192], P(None, 'col'), may hold values from 0 to 1, as said below
- shifts: float32 [16384], P('col'), may hold values from 0 to 4
- source: int32 [16384], P('col'), may hold values from 0 to 16384, as said below
Outputs:
- vectors: float32 [2, 2048, 16384], P(None, 'row', 'col')
- slab_weight: float32 [16384], P('col')
Inputs may be any that keep to these rules, and one draw needn't show every extreme that they name: source[j] = 16384 marks an undeflated merged column; any other value is the pole whose child column the merged column copies, and no pole is named twice. Each device's 512 merged columns hold from 64 to 384 undeflated columns, and some device holds exactly 384. kept_mask is 0 exactly at the poles named in source. Some device of col holds no deflated pole: every pole of both children that it holds is kept. `pole_values`: every pole lies at least 0.4 / 16384 away from every entry of shifts.
All inputs are finite; a program needn't handle non-finite values.
Results may differ from a plain program's by a relative error of at most 0.0003.
Values sent between devices are 32-bit elements; how exact they have to be, the bound alone decides.
A program may use at most 64 MiB of HBM per device.

v0:
```python
import math
import jax
import jax.numpy as jnp
from jax import lax
from jax.sharding import PartitionSpec as P

N1 = 8192
exact_mode = lax.Precision.HIGHEST


def cauchy_block(pole_vals, weights, shift_vals):
    return weights[:, :, None] / (pole_vals[:, :, None] - shift_vals[None, None, :])


def local(upper_panel, lower_panel, pole_values, coupling, kept_mask, shifts, source):
    rows_here = upper_panel.shape[0]
    own_cols = shifts.shape[0]
    weighted = coupling * kept_mask.astype(jnp.float32)
    undeflated = source == 2 * N1
    child_base = jnp.array([0, N1], jnp.int32)
    zeros_acc = jnp.zeros((rows_here, own_cols), jnp.float32)
    pieces = (
        lax.all_gather(upper_panel, "col", axis=1, tiled=True),
        lax.all_gather(lower_panel, "col", axis=1, tiled=True),
        lax.all_gather(pole_values, "col", axis=1, tiled=True),
        lax.all_gather(weighted, "col", axis=1, tiled=True),
    )
    span_cols = math.gcd(pieces[0].shape[1], 1024)

    def advance(number, running):
        window = [
            lax.dynamic_slice_in_dim(member, number * span_cols, span_cols, 1) for member in pieces
        ]
        first_pole = number * span_cols
        cauchy = cauchy_block(window[2], window[3], shifts)
        indices = first_pole + lax.iota(jnp.int32, span_cols)
        one_hot = indices[None, :, None] + child_base[:, None, None] == source[None, None, :]
        basis_tile = jnp.where(undeflated[None, None, :], cauchy, one_hot.astype(jnp.float32))
        upper_acc = running[0] + jnp.dot(
            window[0], basis_tile[0], precision=exact_mode, preferred_element_type=jnp.float32
        )
        lower_acc = running[1] + jnp.dot(
            window[1], basis_tile[1], precision=exact_mode, preferred_element_type=jnp.float32
        )
        return (upper_acc, lower_acc, running[2] + jnp.sum(cauchy * cauchy, axis=(0, 1)))

    upper_acc, lower_acc, norm_sums = lax.fori_loop(
        0,
        pieces[0].shape[1] // span_cols,
        advance,
        (zeros_acc, zeros_acc, jnp.zeros((own_cols,), jnp.float32)),
    )
    scaling = jnp.where(undeflated, lax.rsqrt(norm_sums), 1.0)
    vectors = jnp.stack([upper_acc * scaling[None, :], lower_acc * scaling[None, :]])
    partial_weight = jnp.sum(vectors * vectors, axis=(0, 1))
    slab_weight = lax.psum(partial_weight, "row") / (2 * rows_here * lax.axis_size("row"))
    return (vectors, slab_weight)


def solution(mesh):
    in_specs = (
        P("row", "col"),
        P("row", "col"),
        P(None, "col"),
        P(None, "col"),
        P(None, "col"),
        P("col"),
        P("col"),
    )
    out_specs = (P(None, "row", "col"), P("col"))
    return jax.shard_map(local, mesh=mesh, in_specs=in_specs, out_specs=out_specs, check_vma=False)
```

profile of v0, /device:TPU:1, one launch (start us, length us, event | category | flops | bytes accessed | tf_op | source)
XLA Modules:
  0.0 310.2 jit_solution(16482954497444541827)
XLA Ops:
  8.7 0.7 convert_multiply_fusion
  9.4 41.5 %all_gather.13 = f32[2,8192]{1,0:T(2,128)S(1)} all-gather(f32[2,256]{1,0:T(2,128)S(1)} %convert_multiply_fusion), channel_id=1, replica_groups=mesh['row'=8,'col'=32] {'col'}, dimensions={1}, use_global_device_ids=true | all-gather | bytes 67584 | tf_op jit(solution)/shard_map/all_gather | solution.py:26
  50.9 39.2 %all_gather.14 = f32[2,8192]{1,0:T(2,128)S(1)} all-gather(f32[2,256]{1,0:T(2,128)} %param.12), channel_id=1, replica_groups=mesh['row'=8,'col'=32] {'col'}, dimensions={1}, use_global_device_ids=true | all-gather | bytes 67584 | tf_op jit(solution)/shard_map/all_gather | solution.py:25
  90.8 23.1 %all-gather.3.cloned.1.call-done = f32[256,8192]{1,0:T(8,128)} async-done(((f32[256,256]{1,0:T(8,128)}), f32[256,8192]{1,0:T(8,128)}) %all-gather.3.cloned.1.call-update) | async-done | bytes 8388624 | tf_op jit(solution)/shard_map/all_gather | solution.py:23
  113.9 102.9 %all-gather.5.cloned.1.call-done = f32[256,8192]{1,0:T(8,128)} async-done(((f32[256,256]{1,0:T(8,128)}), f32[256,8192]{1,0:T(8,128)}) %all-gather.5.cloned.1.call-update) | async-done | bytes 8388624 | tf_op jit(solution)/shard_map/all_gather | solution.py:24
  216.8 68.3 %while.18 = (s32[]{:T(128)}, f32[256,512]{1,0:T(8,128)S(1)}, f32[256,512]{1,0:T(8,128)S(1)}, f32[512]{0:T(512)S(1)}, f32[256,8192]{1,0:T(8,128)}, /*index=5*/pre...) while((s32[]{:T(128)}, f32[256,512]{1,0:T(8,128)S(1)}, ...), condition=%wide.region_2.3_spmd.clone, body=%wide.region_0.2_spmd.clone.sunk | while | flops 3229093376 | bytes 12669679 | solution.py:47
  216.9 1.9 multiply_reduce_fusion.3
  218.8 3.3 %fusion.17 = f32[256,512]{1,0:T(8,128)S(1)} fusion(f32[2,1024,512]{2,1,0:T(8,128)S(1)} %get-tuple-element.347, f32[256,8192]{1,0:T(8,128)} %get-tuple-element.389, s32[]{:T(128)S(6)} %select_n.28, f32[256,512]{1,0:T(8,128)S(1)} %get-tuple-element.366, pred[]{:T(512)S(6)} %compare.3), kind=kOutput, calls=%fused_computation.9.clone.1 | convolution fusion | flops 1610874880 | bytes 4194309 | tf_op jit(solution)/shard_map/while/body/eval_jaxpr/dot_general | solution.py:42
  222.1 3.3 %fusion.16 = f32[256,512]{1,0:T(8,128)S(1)} fusion(f32[2,1024,512]{2,1,0:T(8,128)S(1)} %get-tuple-element.347, f32[256,8192]{1,0:T(8,128)} %get-tuple-element.383, s32[]{:T(128)S(6)} %select_n.28, f32[256,512]{1,0:T(8,128)S(1)} %get-tuple-element.365, pred[]{:T(512)S(6)} %compare.3), kind=kOutput, calls=%fused_computation.8.clone.1 | convolution fusion | flops 1610874880 | bytes 4194309 | tf_op jit(solution)/shard_map/while/body/eval_jaxpr/dot_general | solution.py:39
  225.5 1.9 multiply_reduce_fusion.3
  227.4 3.3 %fusion.17 = f32[256,512]{1,0:T(8,128)S(1)} fusion(f32[2,1024,512]{2,1,0:T(8,128)S(1)} %get-tuple-element.347, f32[256,8192]{1,0:T(8,128)} %get-tuple-element.389, s32[]{:T(128)S(6)} %select_n.28, f32[256,512]{1,0:T(8,128)S(1)} %get-tuple-element.366, pred[]{:T(512)S(6)} %compare.3), kind=kOutput, calls=%fused_computation.9.clone.1 | convolution fusion | flops 1610874880 | bytes 4194309 | tf_op jit(solution)/shard_map/while/body/eval_jaxpr/dot_general | solution.py:42
  230.6 3.3 %fusion.16 = f32[256,512]{1,0:T(8,128)S(1)} fusion(f32[2,1024,512]{2,1,0:T(8,128)S(1)} %get-tuple-element.347, f32[256,8192]{1,0:T(8,128)} %get-tuple-element.383, s32[]{:T(128)S(6)} %select_n.28, f32[256,512]{1,0:T(8,128)S(1)} %get-tuple-element.365, pred[]{:T(512)S(6)} %compare.3), kind=kOutput, calls=%fused_computation.8.clone.1 | convolution fusion | flops 1610874880 | bytes 4194309 | tf_op jit(solution)/shard_map/while/body/eval_jaxpr/dot_general | solution.py:39
  234.0 1.9 multiply_reduce_fusion.3
  235.9 3.3 %fusion.17 = f32[256,512]{1,0:T(8,128)S(1)} fusion(f32[2,1024,512]{2,1,0:T(8,128)S(1)} %get-tuple-element.347, f32[256,8192]{1,0:T(8,128)} %get-tuple-element.389, s32[]{:T(128)S(6)} %select_n.28, f32[256,512]{1,0:T(8,128)S(1)} %get-tuple-element.366, pred[]{:T(512)S(6)} %compare.3), kind=kOutput, calls=%fused_computation.9.clone.1 | convolution fusion | flops 1610874880 | bytes 4194309 | tf_op jit(solution)/shard_map/while/body/eval_jaxpr/dot_general | solution.py:42
  239.2 3.3 %fusion.16 = f32[256,512]{1,0:T(8,128)S(1)} fusion(f32[2,1024,512]{2,1,0:T(8,128)S(1)} %get-tuple-element.347, f32[256,8192]{1,0:T(8,128)} %get-tuple-element.383, s32[]{:T(128)S(6)} %select_n.28, f32[256,512]{1,0:T(8,128)S(1)} %get-tuple-element.365, pred[]{:T(512)S(6)} %compare.3), kind=kOutput, calls=%fused_computation.8.clone.1 | convolution fusion | flops 1610874880 | bytes 4194309 | tf_op jit(solution)/shard_map/while/body/eval_jaxpr/dot_general | solution.py:39
  242.6 1.9 multiply_reduce_fusion.3
  244.5 3.3 %fusion.17 = f32[256,512]{1,0:T(8,128)S(1)} fusion(f32[2,1024,512]{2,1,0:T(8,128)S(1)} %get-tuple-element.347, f32[256,8192]{1,0:T(8,128)} %get-tuple-element.389, s32[]{:T(128)S(6)} %select_n.28, f32[256,512]{1,0:T(8,128)S(1)} %get-tuple-element.366, pred[]{:T(512)S(6)} %compare.3), kind=kOutput, calls=%fused_computation.9.clone.1 | convolution fusion | flops 1610874880 | bytes 4194309 | tf_op jit(solution)/shard_map/while/body/eval_jaxpr/dot_general | solution.py:42
  247.7 3.3 %fusion.16 = f32[256,512]{1,0:T(8,128)S(1)} fusion(f32[2,1024,512]{2,1,0:T(8,128)S(1)} %get-tuple-element.347, f32[256,8192]{1,0:T(8,128)} %get-tuple-element.383, s32[]{:T(128)S(6)} %select_n.28, f32[256,512]{1,0:T(8,128)S(1)} %get-tuple-element.365, pred[]{:T(512)S(6)} %compare.3), kind=kOutput, calls=%fused_computation.8.clone.1 | convolution fusion | flops 1610874880 | bytes 4194309 | tf_op jit(solution)/shard_map/while/body/eval_jaxpr/dot_general | solution.py:39
  251.1 1.9 multiply_reduce_fusion.3
  253.0 3.3 %fusion.17 = f32[256,512]{1,0:T(8,128)S(1)} fusion(f32[2,1024,512]{2,1,0:T(8,128)S(1)} %get-tuple-element.347, f32[256,8192]{1,0:T(8,128)} %get-tuple-element.389, s32[]{:T(128)S(6)} %select_n.28, f32[256,512]{1,0:T(8,128)S(1)} %get-tuple-element.366, pred[]{:T(512)S(6)} %compare.3), kind=kOutput, calls=%fused_computation.9.clone.1 | convolution fusion | flops 1610874880 | bytes 4194309 | tf_op jit(solution)/shard_map/while/body/eval_jaxpr/dot_general | solution.py:42
  256.3 3.3 %fusion.16 = f32[256,512]{1,0:T(8,128)S(1)} fusion(f32[2,1024,512]{2,1,0:T(8,128)S(1)} %get-tuple-element.347, f32[256,8192]{1,0:T(8,128)} %get-tuple-element.383, s32[]{:T(128)S(6)} %select_n.28, f32[256,512]{1,0:T(8,128)S(1)} %get-tuple-element.365, pred[]{:T(512)S(6)} %compare.3), kind=kOutput, calls=%fused_computation.8.clone.1 | convolution fusion | flops 1610874880 | bytes 4194309 | tf_op jit(solution)/shard_map/while/body/eval_jaxpr/dot_general | solution.py:39
  259.6 1.9 multiply_reduce_fusion.3
  261.5 3.3 %fusion.17 = f32[256,512]{1,0:T(8,128)S(1)} fusion(f32[2,1024,512]{2,1,0:T(8,128)S(1)} %get-tuple-element.347, f32[256,8192]{1,0:T(8,128)} %get-tuple-element.389, s32[]{:T(128)S(6)} %select_n.28, f32[256,512]{1,0:T(8,128)S(1)} %get-tuple-element.366, pred[]{:T(512)S(6)} %compare.3), kind=kOutput, calls=%fused_computation.9.clone.1 | convolution fusion | flops 1610874880 | bytes 4194309 | tf_op jit(solution)/shard_map/while/body/eval_jaxpr/dot_general | solution.py:42
  264.8 3.3 %fusion.16 = f32[256,512]{1,0:T(8,128)S(1)} fusion(f32[2,1024,512]{2,1,0:T(8,128)S(1)} %get-tuple-element.347, f32[256,8192]{1,0:T(8,128)} %get-tuple-element.383, s32[]{:T(128)S(6)} %select_n.28, f32[256,512]{1,0:T(8,128)S(1)} %get-tuple-element.365, pred[]{:T(512)S(6)} %compare.3), kind=kOutput, calls=%fused_computation.8.clone.1 | convolution fusion | flops 1610874880 | bytes 4194309 | tf_op jit(solution)/shard_map/while/body/eval_jaxpr/dot_general | solution.py:39
  268.2 1.9 multiply_reduce_fusion.3
  270.1 3.3 %fusion.17 = f32[256,512]{1,0:T(8,128)S(1)} fusion(f32[2,1024,512]{2,1,0:T(8,128)S(1)} %get-tuple-element.347, f32[256,8192]{1,0:T(8,128)} %get-tuple-element.389, s32[]{:T(128)S(6)} %select_n.28, f32[256,512]{1,0:T(8,128)S(1)} %get-tuple-element.366, pred[]{:T(512)S(6)} %compare.3), kind=kOutput, calls=%fused_computation.9.clone.1 | convolution fusion | flops 1610874880 | bytes 4194309 | tf_op jit(solution)/shard_map/while/body/eval_jaxpr/dot_general | solution.py:42
  273.3 3.3 %fusion.16 = f32[256,512]{1,0:T(8,128)S(1)} fusion(f32[2,1024,512]{2,1,0:T(8,128)S(1)} %get-tuple-element.347, f32[256,8192]{1,0:T(8,128)} %get-tuple-element.383, s32[]{:T(128)S(6)} %select_n.28, f32[256,512]{1,0:T(8,128)S(1)} %get-tuple-element.365, pred[]{:T(512)S(6)} %compare.3), kind=kOutput, calls=%fused_computation.8.clone.1 | convolution fusion | flops 1610874880 | bytes 4194309 | tf_op jit(solution)/shard_map/while/body/eval_jaxpr/dot_general | solution.py:39
  276.7 1.9 multiply_reduce_fusion.3
  278.6 3.3 %fusion.17 = f32[256,512]{1,0:T(8,128)S(1)} fusion(f32[2,1024,512]{2,1,0:T(8,128)S(1)} %get-tuple-element.347, f32[256,8192]{1,0:T(8,128)} %get-tuple-element.389, s32[]{:T(128)S(6)} %select_n.28, f32[256,512]{1,0:T(8,128)S(1)} %get-tuple-element.366, pred[]{:T(512)S(6)} %compare.3), kind=kOutput, calls=%fused_computation.9.clone.1 | convolution fusion | flops 1610874880 | bytes 4194309 | tf_op jit(solution)/shard_map/while/body/eval_jaxpr/dot_general | solution.py:42
  281.9 3.3 %fusion.16 = f32[256,512]{1,0:T(8,128)S(1)} fusion(f32[2,1024,512]{2,1,0:T(8,128)S(1)} %get-tuple-element.347, f32[256,8192]{1,0:T(8,128)} %get-tuple-element.383, s32[]{:T(128)S(6)} %select_n.28, f32[256,512]{1,0:T(8,128)S(1)} %get-tuple-element.365, pred[]{:T(512)S(6)} %compare.3), kind=kOutput, calls=%fused_computation.8.clone.1 | convolution fusion | flops 1610874880 | bytes 4194309 | tf_op jit(solution)/shard_map/while/body/eval_jaxpr/dot_general | solution.py:39
  286.0 1.1 multiply_reduce_fusion.1
  287.1 15.6 %psum.7 = f32[512]{0:T(512)S(1)} all-reduce(f32[512]{0:T(512)S(1)} %get-tuple-element.266), channel_id=1, replica_groups=mesh['row'=8,'col'=32] {'row'}, use_global_device_ids=true, to_apply=%region_4.5 | all-reduce | flops 512 | bytes 4096 | tf_op jit(solution)/shard_map/psum | solution.py:56
  (51 shorter events, 4.3 us)
Async XLA Ops:
  7.2 106.8 %all-gather.3.cloned.1.call-start = ((), (), s32[]{:S(2)}) async-start(), calls=%async_computation | async-start | bytes 8650752 | tf_op jit(solution)/shard_map/all_gather | solution.py:23
  7.9 209.0 %all-gather.5.cloned.1.call-start = ((), (), s32[]{:S(2)}) async-start(), calls=%async_computation.1 | async-start | bytes 8650752 | tf_op jit(solution)/shard_map/all_gather | solution.py:24
Sparse Core Ops, SparseCore 0:
  10.4 103.4 all-gather.2
  116.4 100.4 all-gather.4
where the time goes:
time: 311 us; the launch traced here: 310 us
  waiting for transfers between devices  127 us (41%)
  blocking collectives  96.3 us (31%)
  matrix products  52.1 us (17%)
  other arithmetic  19.7 us (6%)
  between operations  14.1 us (5%)
    all_gather x1, waiting for transfers between devices, local(): lax.all_gather(lower_panel, 'col', axis=1, tiled=True)  103 us
    all_gather x1, blocking collectives, local(): lax.all_gather(weighted, 'col', axis=1, tiled=True)  41.5 us
    all_gather x1, blocking collectives, local(): lax.all_gather(pole_values, 'col', axis=1, tiled=True)  39.2 us
    dot_general x8, matrix products, advance(): jnp.dot(window[0], basis_tile[0], precision=exact_mode, preferred_element...  26 us
    dot_general x8, matrix products, advance(): jnp.dot(window[1], basis_tile[1], precision=exact_mode, preferred_element...  26 us
    all_gather x1, waiting for transfers between devices, local(): lax.all_gather(upper_panel, 'col', axis=1, tiled=True)  23.1 us
    psum x1, blocking collectives, local(): lax.psum(partial_weight, 'row') / (2 * rows_here * lax.axis_size('row'))  15.6 us
    reduce_sum x8, other arithmetic, advance(): jnp.sum(cauchy * cauchy, axis=(0, 1))  15 us
  transfers between devices with their start and end apart: 2, of which 2 were waited for; matrix products, arithmetic and copies ran while one was open for 0% of the time, Pallas kernels for 0%

commit v1 on v0

--- a/solution.py
+++ b/solution.py
@@ -22,7 +22,7 @@
     pieces = (
         lax.all_gather(upper_panel, "col", axis=1, tiled=True),
         lax.all_gather(lower_panel, "col", axis=1, tiled=True),
-        lax.all_gather(pole_values, "col", axis=1, tiled=True),
+        jnp.concatenate(lax.all_gather(pole_values, "col"), 1),
         lax.all_gather(weighted, "col", axis=1, tiled=True),
     )
     span_cols = math.gcd(pieces[0].shape[1], 1024)

time: 311 us -> 311 us (level)
  no operation moved by 1% of the time
where the time goes in v1:
time: 311 us; the launch traced here: 310 us
  waiting for transfers between devices  127 us (41%)
  blocking collectives  96.3 us (31%)
  matrix products  52.1 us (17%)
  other arithmetic  19.7 us (6%)
  between operations  14.1 us (5%)
    all_gather x1, waiting for transfers between devices, local(): lax.all_gather(lower_panel, 'col', axis=1, tiled=True)  103 us
    all_gather x1, blocking collectives, local(): lax.all_gather(weighted, 'col', axis=1, tiled=True)  41.5 us
    all_gather x1, blocking collectives, local(): lax.all_gather(pole_values, 'col')  39.2 us
    dot_general x8, matrix products, advance(): jnp.dot(window[0], basis_tile[0], precision=exact_mode, preferred_element...  26 us
    dot_general x8, matrix products, advance(): jnp.dot(window[1], basis_tile[1], precision=exact_mode, preferred_element...  26 us
    all_gather x1, waiting for transfers between devices, local(): lax.all_gather(upper_panel, 'col', axis=1, tiled=True)  23.1 us
    psum x1, blocking collectives, local(): lax.psum(partial_weight, 'row') / (2 * rows_here * lax.axis_size('row'))  15.6 us
    reduce_sum x8, other arithmetic, advance(): jnp.sum(cauchy * cauchy, axis=(0, 1))  15 us
  transfers between devices with their start and end apart: 2, of which 2 were waited for; matrix products, arithmetic and copies ran while one was open for 0% of the time, Pallas kernels for 0%

profile of v1, /device:TPU:1, one launch (start us, length us, event | category | flops | bytes accessed | tf_op | source)
XLA Modules:
  0.0 310.2 jit_solution(5609160749761621071)
XLA Ops:
  8.7 0.7 convert_multiply_fusion
  9.4 41.5 %all_gather.16 = f32[2,8192]{1,0:T(2,128)S(1)} all-gather(f32[2,256]{1,0:T(2,128)S(1)} %convert_multiply_fusion), channel_id=1, replica_groups=mesh['row'=8,'col'=32] {'col'}, dimensions={1}, use_global_device_ids=true | all-gather | bytes 67584 | tf_op jit(solution)/shard_map/all_gather | solution.py:26
  50.9 39.2 %all-gather.1 = f32[32,2,256]{2,1,0:T(2,128)S(1)} all-gather(f32[1,2,256]{2,1,0:T(2,128)} %bitcast.23), channel_id=2, replica_groups=mesh['row'=8,'col'=32] {'col'}, dimensions={0}, use_global_device_ids=true | all-gather | bytes 67584 | tf_op jit(solution)/shard_map/all_gather | solution.py:25
  90.8 23.1 %all-gather.5.cloned.1.call-done = f32[256,8192]{1,0:T(8,128)} async-done(((f32[256,256]{1,0:T(8,128)}), f32[256,8192]{1,0:T(8,128)}) %all-gather.5.cloned.1.call-update) | async-done | bytes 8388624 | tf_op jit(solution)/shard_map/all_gather | solution.py:23
  113.9 102.9 %all-gather.7.cloned.1.call-done = f32[256,8192]{1,0:T(8,128)} async-done(((f32[256,256]{1,0:T(8,128)}), f32[256,8192]{1,0:T(8,128)}) %all-gather.7.cloned.1.call-update) | async-done | bytes 8388624 | tf_op jit(solution)/shard_map/all_gather | solution.py:24
  216.8 68.3 %while.18 = (s32[]{:T(128)}, f32[256,512]{1,0:T(8,128)S(1)}, f32[256,512]{1,0:T(8,128)S(1)}, f32[512]{0:T(512)S(1)}, f32[256,8192]{1,0:T(8,128)}, /*index=5*/pre...) while((s32[]{:T(128)}, f32[256,512]{1,0:T(8,128)S(1)}, ...), condition=%wide.region_2.3_spmd.clone, body=%wide.region_0.2_spmd.clone.sunk | while | flops 3229093376 | bytes 12669679 | solution.py:47
  216.9 1.9 multiply_reduce_fusion.3
  218.8 3.3 %fusion.17 = f32[256,512]{1,0:T(8,128)S(1)} fusion(f32[2,1024,512]{2,1,0:T(8,128)S(1)} %get-tuple-element.347, f32[256,8192]{1,0:T(8,128)} %get-tuple-element.389, s32[]{:T(128)S(6)} %select_n.28, f32[256,512]{1,0:T(8,128)S(1)} %get-tuple-element.366, pred[]{:T(512)S(6)} %compare.3), kind=kOutput, calls=%fused_computation.9.clone.1 | convolution fusion | flops 1610874880 | bytes 4194309 | tf_op jit(solution)/shard_map/while/body/eval_jaxpr/dot_general | solution.py:42
  222.1 3.3 %fusion.16 = f32[256,512]{1,0:T(8,128)S(1)} fusion(f32[2,1024,512]{2,1,0:T(8,128)S(1)} %get-tuple-element.347, f32[256,8192]{1,0:T(8,128)} %get-tuple-element.383, s32[]{:T(128)S(6)} %select_n.28, f32[256,512]{1,0:T(8,128)S(1)} %get-tuple-element.365, pred[]{:T(512)S(6)} %compare.3), kind=kOutput, calls=%fused_computation.8.clone.1 | convolution fusion | flops 1610874880 | bytes 4194309 | tf_op jit(solution)/shard_map/while/body/eval_jaxpr/dot_general | solution.py:39
  225.5 1.9 multiply_reduce_fusion.3
  227.4 3.3 %fusion.17 = f32[256,512]{1,0:T(8,128)S(1)} fusion(f32[2,1024,512]{2,1,0:T(8,128)S(1)} %get-tuple-element.347, f32[256,8192]{1,0:T(8,128)} %get-tuple-element.389, s32[]{:T(128)S(6)} %select_n.28, f32[256,512]{1,0:T(8,128)S(1)} %get-tuple-element.366, pred[]{:T(512)S(6)} %compare.3), kind=kOutput, calls=%fused_computation.9.clone.1 | convolution fusion | flops 1610874880 | bytes 4194309 | tf_op jit(solution)/shard_map/while/body/eval_jaxpr/dot_general | solution.py:42
  230.6 3.3 %fusion.16 = f32[256,512]{1,0:T(8,128)S(1)} fusion(f32[2,1024,512]{2,1,0:T(8,128)S(1)} %get-tuple-element.347, f32[256,8192]{1,0:T(8,128)} %get-tuple-element.383, s32[]{:T(128)S(6)} %select_n.28, f32[256,512]{1,0:T(8,128)S(1)} %get-tuple-element.365, pred[]{:T(512)S(6)} %compare.3), kind=kOutput, calls=%fused_computation.8.clone.1 | convolution fusion | flops 1610874880 | bytes 4194309 | tf_op jit(solution)/shard_map/while/body/eval_jaxpr/dot_general | solution.py:39
  234.0 1.9 multiply_reduce_fusion.3
  235.9 3.3 %fusion.17 = f32[256,512]{1,0:T(8,128)S(1)} fusion(f32[2,1024,512]{2,1,0:T(8,128)S(1)} %get-tuple-element.347, f32[256,8192]{1,0:T(8,128)} %get-tuple-element.389, s32[]{:T(128)S(6)} %select_n.28, f32[256,512]{1,0:T(8,128)S(1)} %get-tuple-element.366, pred[]{:T(512)S(6)} %compare.3), kind=kOutput, calls=%fused_computation.9.clone.1 | convolution fusion | flops 1610874880 | bytes 4194309 | tf_op jit(solution)/shard_map/while/body/eval_jaxpr/dot_general | solution.py:42
  239.2 3.3 %fusion.16 = f32[256,512]{1,0:T(8,128)S(1)} fusion(f32[2,1024,512]{2,1,0:T(8,128)S(1)} %get-tuple-element.347, f32[256,8192]{1,0:T(8,128)} %get-tuple-element.383, s32[]{:T(128)S(6)} %select_n.28, f32[256,512]{1,0:T(8,128)S(1)} %get-tuple-element.365, pred[]{:T(512)S(6)} %compare.3), kind=kOutput, calls=%fused_computation.8.clone.1 | convolution fusion | flops 1610874880 | bytes 4194309 | tf_op jit(solution)/shard_map/while/body/eval_jaxpr/dot_general | solution.py:39
  242.6 1.9 multiply_reduce_fusion.3
  244.5 3.3 %fusion.17 = f32[256,512]{1,0:T(8,128)S(1)} fusion(f32[2,1024,512]{2,1,0:T(8,128)S(1)} %get-tuple-element.347, f32[256,8192]{1,0:T(8,128)} %get-tuple-element.389, s32[]{:T(128)S(6)} %select_n.28, f32[256,512]{1,0:T(8,128)S(1)} %get-tuple-element.366, pred[]{:T(512)S(6)} %compare.3), kind=kOutput, calls=%fused_computation.9.clone.1 | convolution fusion | flops 1610874880 | bytes 4194309 | tf_op jit(solution)/shard_map/while/body/eval_jaxpr/dot_general | solution.py:42
  247.7 3.3 %fusion.16 = f32[256,512]{1,0:T(8,128)S(1)} fusion(f32[2,1024,512]{2,1,0:T(8,128)S(1)} %get-tuple-element.347, f32[256,8192]{1,0:T(8,128)} %get-tuple-element.383, s32[]{:T(128)S(6)} %select_n.28, f32[256,512]{1,0:T(8,128)S(1)} %get-tuple-element.365, pred[]{:T(512)S(6)} %compare.3), kind=kOutput, calls=%fused_computation.8.clone.1 | convolution fusion | flops 1610874880 | bytes 4194309 | tf_op jit(solution)/shard_map/while/body/eval_jaxpr/dot_general | solution.py:39
  251.1 1.9 multiply_reduce_fusion.3
  253.0 3.3 %fusion.17 = f32[256,512]{1,0:T(8,128)S(1)} fusion(f32[2,1024,512]{2,1,0:T(8,128)S(1)} %get-tuple-element.347, f32[256,8192]{1,0:T(8,128)} %get-tuple-element.389, s32[]{:T(128)S(6)} %select_n.28, f32[256,512]{1,0:T(8,128)S(1)} %get-tuple-element.366, pred[]{:T(512)S(6)} %compare.3), kind=kOutput, calls=%fused_computation.9.clone.1 | convolution fusion | flops 1610874880 | bytes 4194309 | tf_op jit(solution)/shard_map/while/body/eval_jaxpr/dot_general | solution.py:42
  256.3 3.3 %fusion.16 = f32[256,512]{1,0:T(8,128)S(1)} fusion(f32[2,1024,512]{2,1,0:T(8,128)S(1)} %get-tuple-element.347, f32[256,8192]{1,0:T(8,128)} %get-tuple-element.383, s32[]{:T(128)S(6)} %select_n.28, f32[256,512]{1,0:T(8,128)S(1)} %get-tuple-element.365, pred[]{:T(512)S(6)} %compare.3), kind=kOutput, calls=%fused_computation.8.clone.1 | convolution fusion | flops 1610874880 | bytes 4194309 | tf_op jit(solution)/shard_map/while/body/eval_jaxpr/dot_general | solution.py:39
  259.6 1.9 multiply_reduce_fusion.3
  261.5 3.3 %fusion.17 = f32[256,512]{1,0:T(8,128)S(1)} fusion(f32[2,1024,512]{2,1,0:T(8,128)S(1)} %get-tuple-element.347, f32[256,8192]{1,0:T(8,128)} %get-tuple-element.389, s32[]{:T(128)S(6)} %select_n.28, f32[256,512]{1,0:T(8,128)S(1)} %get-tuple-element.366, pred[]{:T(512)S(6)} %compare.3), kind=kOutput, calls=%fused_computation.9.clone.1 | convolution fusion | flops 1610874880 | bytes 4194309 | tf_op jit(solution)/shard_map/while/body/eval_jaxpr/dot_general | solution.py:42
  264.8 3.3 %fusion.16 = f32[256,512]{1,0:T(8,128)S(1)} fusion(f32[2,1024,512]{2,1,0:T(8,128)S(1)} %get-tuple-element.347, f32[256,8192]{1,0:T(8,128)} %get-tuple-element.383, s32[]{:T(128)S(6)} %select_n.28, f32[256,512]{1,0:T(8,128)S(1)} %get-tuple-element.365, pred[]{:T(512)S(6)} %compare.3), kind=kOutput, calls=%fused_computation.8.clone.1 | convolution fusion | flops 1610874880 | bytes 4194309 | tf_op jit(solution)/shard_map/while/body/eval_jaxpr/dot_general | solution.py:39
  268.2 1.9 multiply_reduce_fusion.3
  270.1 3.3 %fusion.17 = f32[256,512]{1,0:T(8,128)S(1)} fusion(f32[2,1024,512]{2,1,0:T(8,128)S(1)} %get-tuple-element.347, f32[256,8192]{1,0:T(8,128)} %get-tuple-element.389, s32[]{:T(128)S(6)} %select_n.28, f32[256,512]{1,0:T(8,128)S(1)} %get-tuple-element.366, pred[]{:T(512)S(6)} %compare.3), kind=kOutput, calls=%fused_computation.9.clone.1 | convolution fusion | flops 1610874880 | bytes 4194309 | tf_op jit(solution)/shard_map/while/body/eval_jaxpr/dot_general | solution.py:42
  273.3 3.3 %fusion.16 = f32[256,512]{1,0:T(8,128)S(1)} fusion(f32[2,1024,512]{2,1,0:T(8,128)S(1)} %get-tuple-element.347, f32[256,8192]{1,0:T(8,128)} %get-tuple-element.383, s32[]{:T(128)S(6)} %select_n.28, f32[256,512]{1,0:T(8,128)S(1)} %get-tuple-element.365, pred[]{:T(512)S(6)} %compare.3), kind=kOutput, calls=%fused_computation.8.clone.1 | convolution fusion | flops 1610874880 | bytes 4194309 | tf_op jit(solution)/shard_map/while/body/eval_jaxpr/dot_general | solution.py:39
  276.7 1.9 multiply_reduce_fusion.3
  278.6 3.3 %fusion.17 = f32[256,512]{1,0:T(8,128)S(1)} fusion(f32[2,1024,512]{2,1,0:T(8,128)S(1)} %get-tuple-element.347, f32[256,8192]{1,0:T(8,128)} %get-tuple-element.389, s32[]{:T(128)S(6)} %select_n.28, f32[256,512]{1,0:T(8,128)S(1)} %get-tuple-element.366, pred[]{:T(512)S(6)} %compare.3), kind=kOutput, calls=%fused_computation.9.clone.1 | convolution fusion | flops 1610874880 | bytes 4194309 | tf_op jit(solution)/shard_map/while/body/eval_jaxpr/dot_general | solution.py:42
  281.9 3.3 %fusion.16 = f32[256,512]{1,0:T(8,128)S(1)} fusion(f32[2,1024,512]{2,1,0:T(8,128)S(1)} %get-tuple-element.347, f32[256,8192]{1,0:T(8,128)} %get-tuple-element.383, s32[]{:T(128)S(6)} %select_n.28, f32[256,512]{1,0:T(8,128)S(1)} %get-tuple-element.365, pred[]{:T(512)S(6)} %compare.3), kind=kOutput, calls=%fused_computation.8.clone.1 | convolution fusion | flops 1610874880 | bytes 4194309 | tf_op jit(solution)/shard_map/while/body/eval_jaxpr/dot_general | solution.py:39
  286.0 1.1 multiply_reduce_fusion.1
  287.1 15.6 %psum.7 = f32[512]{0:T(512)S(1)} all-reduce(f32[512]{0:T(512)S(1)} %get-tuple-element.266), channel_id=1, replica_groups=mesh['row'=8,'col'=32] {'row'}, use_global_device_ids=true, to_apply=%region_4.5 | all-reduce | flops 512 | bytes 4096 | tf_op jit(solution)/shard_map/psum | solution.py:56
  (51 shorter events, 4.3 us)
Async XLA Ops:
  7.2 106.8 %all-gather.5.cloned.1.call-start = ((), (), s32[]{:S(2)}) async-start(), calls=%async_computation | async-start | bytes 8650752 | tf_op jit(solution)/shard_map/all_gather | solution.py:23
  7.9 209.0 %all-gather.7.cloned.1.call-start = ((), (), s32[]{:S(2)}) async-start(), calls=%async_computation.1 | async-start | bytes 8650752 | tf_op jit(solution)/shard_map/all_gather | solution.py:24
Sparse Core Ops, SparseCore 0:
  10.4 103.4 all-gather.4
  116.4 100.4 all-gather.6
